TPU v7x, 128 devices: a whole 4x4x4 slice. The times are simulated.
128 devices in a mesh: dp: 8 (over x, core), context: 16 (over z, y).
Axes of the slice: x: 4, y: 4, z: 4, core: 2. Of those that a mesh axis runs over, the one named last changes fastest.
Arguments:
- queries: bfloat16 [8, 5120, 4096], P('dp', 'context'), may hold values from -6 to 6
- keys: bfloat16 [8, 5120, 4096], P('dp', 'context'), may hold values from -6 to 6
- values: bfloat16 [8, 5120, 4096], P('dp', 'context'), may hold values from -6 to 6
- gain: float32 [4096], replicated, may hold values from 0.1 to 1.9
- out_grad: bfloat16 [8, 5120, 4096], P('dp', 'context'), may hold values from -6 to 6
Outputs:
- output: bfloat16 [8, 5120, 4096], P('dp', 'context')
- query_grad: bfloat16 [8, 5120, 4096], P('dp', 'context')
- key_grad: bfloat16 [8, 5120, 4096], P('dp', 'context')
- value_grad: bfloat16 [8, 5120, 4096], P('dp', 'context')
- gain_grad: float32 [4096], replicated
All inputs are finite; a program needn't handle non-finite values.
Results may differ from a plain program's by a relative error of at most 0.0064.
Values may be sent and summed in bfloat16 or wider, within the bound.
A program may use at most 192 MiB of HBM per device.

v0:
```python
import jax
import jax.numpy as jnp
from jax import lax
from jax.sharding import PartitionSpec as P

HEADS = 32
HD = 128


epsilon = 1e-06


def carried_in(array, axis, join, neutral, backward):
    count = lax.axis_size(axis)
    place = lax.axis_index(axis)
    ahead = count - 1 - place if backward else place
    gathered = lax.all_gather(array.astype(jnp.bfloat16), axis)
    state = jnp.zeros_like(array) + jnp.asarray(neutral, array.dtype)

    def one(hop, state):
        source = count - 1 - hop if backward else hop
        return join(state, lax.dynamic_index_in_dim(gathered, source, 0, False).astype(array.dtype))

    return lax.fori_loop(0, ahead, one, state)


def add_states(earlier, later_one):
    return earlier + later_one


def shards(queries, keys, values, gain, out_grad):
    tok_rows = queries.shape[1]
    local_query_rows = queries[0].reshape(tok_rows, HEADS, HD)
    local_key_rows = keys[0].reshape(tok_rows, HEADS, HD)
    local_value_rows = values[0].reshape(tok_rows, HEADS, HD)
    zero_state = jnp.zeros((HEADS, HD, HD), jnp.float32)
    causal = lax.broadcasted_iota(jnp.int32, (tok_rows, tok_rows), 0) >= lax.broadcasted_iota(
        jnp.int32, (tok_rows, tok_rows), 1
    )
    block_state = jnp.einsum(
        "uwc,uwg->wcg", local_key_rows, local_value_rows, preferred_element_type=jnp.float32
    ).astype(jnp.bfloat16)
    prior_state = carried_in(
        block_state.astype(jnp.float32), "context", add_states, zero_state, False
    )
    preceding_block = prior_state.astype(jnp.bfloat16)
    scores = jnp.einsum(
        "thk,shk->hts", local_query_rows, local_key_rows, preferred_element_type=jnp.float32
    )
    attn_weights = jnp.where(causal, scores, 0.0).astype(jnp.bfloat16)
    mixed_out = jnp.einsum(
        "hts,shv->thv", attn_weights, local_value_rows, preferred_element_type=jnp.float32
    )
    mixed_out = mixed_out + jnp.einsum(
        "lyq,yqd->lyd", local_query_rows, preceding_block, preferred_element_type=jnp.float32
    )
    mixed_out = mixed_out.reshape(tok_rows, HEADS * HD)
    inv_rms = lax.rsqrt(jnp.mean(mixed_out * mixed_out, -1, keepdims=True) + epsilon)
    normed = mixed_out * inv_rms
    output = (normed * gain).astype(jnp.bfloat16)
    grad_out = out_grad[0].astype(jnp.float32)
    gain_part = jnp.sum(grad_out * normed, 0)
    scaled = gain * grad_out
    centered_input = jnp.mean(scaled * mixed_out, -1, keepdims=True)
    mixed_gradient = (
        inv_rms * scaled - mixed_out * inv_rms * inv_rms * inv_rms * centered_input
    ).astype(jnp.bfloat16)
    mixed_gradient = mixed_gradient.reshape(tok_rows, HEADS, HD)
    state_grad = jnp.einsum(
        "uwc,uwg->wcg", local_query_rows, mixed_gradient, preferred_element_type=jnp.float32
    ).astype(jnp.bfloat16)
    later_state = carried_in(
        state_grad.astype(jnp.float32), "context", add_states, zero_state, True
    )
    following_block = later_state.astype(jnp.bfloat16)
    d_scores = jnp.einsum(
        "thv,shv->hts", mixed_gradient, local_value_rows, preferred_element_type=jnp.float32
    )
    d_weights = jnp.where(causal, d_scores, 0.0).astype(jnp.bfloat16)
    query_grad = jnp.einsum(
        "hts,shk->thk", d_weights, local_key_rows, preferred_element_type=jnp.float32
    )
    query_grad = query_grad + jnp.einsum(
        "mqy,qsy->mqs", mixed_gradient, preceding_block, preferred_element_type=jnp.float32
    )
    key_grad = jnp.einsum(
        "hts,thk->shk", d_weights, local_query_rows, preferred_element_type=jnp.float32
    )
    key_grad = key_grad + jnp.einsum(
        "mqy,qsy->mqs", local_value_rows, following_block, preferred_element_type=jnp.float32
    )
    value_grad = jnp.einsum(
        "hts,thv->shv", attn_weights, mixed_gradient, preferred_element_type=jnp.float32
    )
    value_grad = value_grad + jnp.einsum(
        "lyq,yqd->lyd", local_key_rows, following_block, preferred_element_type=jnp.float32
    )
    gain_grad = lax.psum(gain_part, ("dp", "context"))
    flat = (1, tok_rows, HEADS * HD)
    return (
        output[None],
        query_grad.reshape(flat).astype(jnp.bfloat16),
        key_grad.reshape(flat).astype(jnp.bfloat16),
        value_grad.reshape(flat).astype(jnp.bfloat16),
        gain_grad,
    )


def solution(mesh):
    in_specs = (
        P("dp", "context", None),
        P("dp", "context", None),
        P("dp", "context", None),
        P(),
        P("dp", "context", None),
    )
    out_specs = (
        P("dp", "context", None),
        P("dp", "context", None),
        P("dp", "context", None),
        P("dp", "context", None),
        P(),
    )
    return jax.shard_map(shards, mesh=mesh, in_specs=in_specs, out_specs=out_specs, check_vma=False)
```

profile of v0, /device:TPU:1, one launch (start us, length us, event | category | flops | bytes accessed | tf_op | source)
XLA Modules:
  0.0 361.7 jit_solution(2841222020369085252)
XLA Ops:
  7.2 2.5 copy.71
  10.4 0.8 copy-done.10
  11.2 4.7 %fusion.26 = bf16[32,128,128]{2,1,0:T(8,128)(2,1)} fusion(bf16[320,32,128]{2,1,0:T(8,128)(2,1)S(1)} %bitcast.75, bf16[320,32,128]{2,1,0:T(8,128)(2,1)S(1)} %bitcast.79), kind=kOutput, calls=%fused_computation.40 | convolution fusion | flops 336068608 | bytes 6291456 | tf_op jit(solution)/shard_map/uwc,uwg->wcg/dot_general | solution.py:40
  16.3 2.5 copy.70
  19.5 3.4 copy.73
  22.9 9.2 %select_convert_fusion.1 = bf16[32,320,320]{2,1,0:T(8,128)(2,1)S(1)} fusion(pred[320,320]{1,0:T(8,128)(4,1)S(1)} %iota_compare_fusion, bf16[320,32,128]{2,1,0:T(8,128)(2,1)} %bitcast.80, bf16[320,32,128]{2,1,0:T(8,128)(2,1)S(1)} %bitcast.71), kind=kOutput, calls=%fused_computation.3 | convolution fusion | flops 845414400 | bytes 11898880 | tf_op jit(solution)/shard_map/thk,shk->hts/dot_general | solution.py:47
  32.1 3.0 copy-done.7
  35.2 5.3 %fusion.9 = f32[32,320,128]{2,1,0:T(8,128)} fusion(bf16[32,320,320]{2,1,0:T(8,128)(2,1)S(1)} %select_convert_fusion.1, bf16[320,32,128]{2,1,0:T(8,128)(2,1)S(1)} %bitcast.76), kind=kOutput, calls=%fused_computation.25 | convolution fusion | flops 838860800 | bytes 14417920 | tf_op jit(solution)/shard_map/hts,shv->thv/dot_general | solution.py:51
  40.5 90.0 %all-gather.5.cloned.1.call-done = bf16[512,128,128]{2,1,0:T(8,128)(2,1)} async-done(((bf16[32,128,128]{2,1,0:T(8,128)(2,1)}), bf16[512,128,128]{2,1,0:T(8,128)(2,1)}) %all-gather.5.cloned.1.call-update) | async-done | bytes 16777232 | tf_op jit(solution)/shard_map/all_gather | solution.py:17
  131.4 9.7 %multiply_reduce_fusion = (f32[320]{0:T(512)S(1)}, f32[320]{0:T(512)S(1)}, f32[320,32,128]{2,0,1:T(8,128)S(1)}) fusion(f32[320,32,128]{2,1,0:T(8,128)} %bitcast.67, f32[32,128]{1,0:T(8,128)S(1)} %bitcast.88, f32[32,128,128]{2,1,0:T(8,128)S(1)} %get-tuple-element.84, bf16[320,32,128]{2,1,0:T(8,128)(2,1)} %bitcast.72, f32[32,320,128]{2,1,0:T(8,128)} %fusion.9), kind=kOutput, calls=%fused_computation.17 | convolution fusion | flops 343932288 | bytes 20466176 | tf_op jit(solution)/shard_map/lyq,yqd->lyd/dot_general | solution.py:54
  141.2 3.8 %subtract_convert_fusion = bf16[320,32,128]{2,0,1:T(8,128)(2,1)S(1)} fusion(f32[320,32,128]{2,0,1:T(8,128)S(1)} %get-tuple-element.112, f32[320,32,128]{2,1,0:T(8,128)S(1)} %bitcast.70, f32[320]{0:T(512)S(1)} %broadcast_multiply_fusion, f32[32,128]{1,0:T(8,128)S(1)} %bitcast.89, f32[320]{0:T(512)S(1)} %add_rsqrt_fusion), kind=kLoop, calls=%fused_computation.16 | loop fusion | flops 10485760 | bytes 13126144 | tf_op jit(solution)/shard_map/convert_element_type | solution.py:67
  145.1 1.5 copy-done.1
  146.6 3.3 fusion.31
  149.9 1.3 copy.60
  151.3 7.9 %copy.52 = f32[320,32,128]{2,1,0:T(8,128)} copy(f32[320,32,128]{2,0,1:T(8,128)} %copy-done) | data formatting | bytes 10485760 | tf_op jit(solution)/shard_map/add | solution.py:54
  159.1 7.0 %reshape.170 = f32[1,320,4096]{2,1,0:T(8,128)} reshape(f32[320,32,128]{2,1,0:T(8,128)} %copy.52) | data formatting | bytes 10485760 | tf_op jit(solution)/shard_map/reshape | solution.py:57
  166.2 6.3 %select_convert_fusion = bf16[32,320,320]{2,1,0:T(8,128)(2,1)S(1)} fusion(bf16[320,32,128]{2,0,1:T(8,128)(2,1)} %copy-done.1, pred[320,320]{1,0:T(8,128)(4,1)S(1)} %iota_compare_fusion, bf16[320,32,128]{2,1,0:T(8,128)(2,1)} %bitcast.77), kind=kOutput, calls=%fused_computation.2 | convolution fusion | flops 845414400 | bytes 11898880 | tf_op jit(solution)/shard_map/thv,shv->hts/dot_general | solution.py:76
  172.5 3.4 fusion.13
  176.1 1.0 fusion.3
  177.1 1.7 copy.56
  178.8 3.1 convert_element_type.121
  181.9 4.4 %fusion.1 = f32[4096]{0:T(1024)S(1)} fusion(bf16[1,320,4096]{2,1,0:T(8,128)(2,1)} %param.13, f32[320]{0:T(512)S(1)} %add_rsqrt_fusion, f32[320,32,128]{2,0,1:T(8,128)} %copy-done), kind=kLoop, calls=%fused_computation.7 | loop fusion | flops 5238784 | bytes 7881984 | tf_op jit(solution)/shard_map/reduce_sum | solution.py:62
  186.2 95.7 %psum.7 = f32[4096]{0:T(1024)} all-reduce(f32[4096]{0:T(1024)S(1)} %fusion.1), channel_id=1, replica_groups=mesh['dp'=8,'context'=16] {'dp','context'}, use_global_device_ids=true, to_apply=%region_7.8 | all-reduce | flops 4096 | bytes 32768 | tf_op jit(solution)/shard_map/psum | solution.py:98
  282.0 9.6 %fusion.19 = f32[32,320,128]{2,1,0:T(8,128)} fusion(bf16[32,320,320]{2,1,0:T(8,128)(2,1)} %copy-done.8, bf16[320,32,128]{2,1,0:T(8,128)(2,1)S(1)} %bitcast.74), kind=kOutput, calls=%fused_computation.35 | convolution fusion | flops 838860800 | bytes 14417920 | tf_op jit(solution)/shard_map/hts,thk->shk/dot_general | solution.py:86
  291.6 4.7 %multiply_convert_fusion = bf16[1,320,4096]{2,1,0:T(8,128)(2,1)} fusion(f32[1,320,4096]{2,1,0:T(8,128)} %reshape.170, f32[4096]{0:T(1024)S(1)} %copy-done.14, f32[320]{0:T(512)S(1)} %add_rsqrt_fusion), kind=kLoop, calls=%fused_computation.18 | loop fusion | flops 3932160 | bytes 7881984 | tf_op jit(solution)/shard_map/convert_element_type | solution.py:60
  296.6 27.0 %while.23 = (s32[]{:T(128)}, f32[32,128,128]{2,1,0:T(8,128)S(1)}, s32[]{:T(128)}, bf16[16,32,128,128]{3,2,1,0:T(8,128)(2,1)}, s32[]{:T(128)}, /*index=5*/s32[]{:T(128)}, s32[]{:T(128)}, s32[]{:T(128)}) while((s32[]{:T(128)}, f32[32,128,128]{2,1,0:T(8,128)S(1)}, s32[]{:T(128)}, bf16[16,32,128,128]{3,2,1,0:T(8,128)(2,1)}, s32[]{:T(128)}, ...), condition=%wide.region_5.6_spmd, body=%wide.region_4.5_spmd.sunk | while | flops 1048582 | bytes 5243023 | solution.py:24
  296.6 1.7 convert_add_fusion.5
  298.4 1.7 convert_add_fusion.5
  300.1 1.7 convert_add_fusion.5
  301.9 1.7 convert_add_fusion.5
  303.7 1.7 convert_add_fusion.5
  305.4 1.7 convert_add_fusion.5
  307.2 1.7 convert_add_fusion.5
  309.0 1.7 convert_add_fusion.5
  310.7 1.7 convert_add_fusion.5
  312.5 1.7 convert_add_fusion.5
  314.3 1.7 convert_add_fusion.5
  316.1 1.7 convert_add_fusion.5
  317.8 1.7 convert_add_fusion.5
  319.6 1.7 convert_add_fusion.5
  321.4 1.7 convert_add_fusion.5
  323.6 5.7 %fusion.11 = f32[32,128,320]{1,2,0:T(8,128)} fusion(bf16[320,32,128]{2,1,0:T(8,128)(2,1)} %bitcast.81, f32[32,128,128]{2,1,0:T(8,128)S(1)} %get-tuple-element.85), kind=kOutput, calls=%fused_computation.27 | convolution fusion | flops 336068608 | bytes 9961472 | tf_op jit(solution)/shard_map/lyq,yqd->lyd/dot_general | solution.py:95
  329.3 7.3 %fusion.4 = bf16[320,32,128]{2,0,1:T(8,128)(2,1)S(1)} fusion(f32[32,128,320]{1,2,0:T(8,128)} %fusion.11, bf16[320,32,128]{2,0,1:T(8,128)(2,1)S(1)} %copy-done.3, bf16[32,320,320]{2,1,0:T(8,128)(2,1)} %copy-done.7), kind=kOutput, calls=%fused_computation.20 | convolution fusion | flops 841482240 | bytes 17039360 | tf_op jit(solution)/shard_map/hts,thv->shv/dot_general | solution.py:92
  336.6 3.2 copy.65
  339.8 5.2 %convert_element_type.129 = bf16[1,320,4096]{2,1,0:T(8,128)(2,1)} reshape(bf16[320,32,128]{2,1,0:T(8,128)(2,1)} %copy.65) | data formatting | bytes 5242880 | tf_op jit(solution)/shard_map/convert_element_type | solution.py:104
  345.0 4.9 %fusion.2 = bf16[320,32,128]{2,0,1:T(8,128)(2,1)S(1)} fusion(f32[32,320,128]{2,1,0:T(8,128)} %fusion.19, bf16[320,32,128]{2,1,0:T(8,128)(2,1)} %bitcast.78, f32[32,128,128]{2,1,0:T(8,128)S(1)} %get-tuple-element.85), kind=kOutput, calls=%fused_computation.10 | convolution fusion | flops 338690048 | bytes 12582912 | tf_op jit(solution)/shard_map/mqy,qsy->mqs/dot_general | solution.py:89
  349.9 1.7 copy.62
  351.6 3.1 convert_element_type.126
  (45 shorter events, 3.2 us)
Async XLA Ops:
  7.2 123.3 %all-gather.5.cloned.1.call-start = ((), (), s32[]{:S(2)}) async-start(), calls=%async_computation | async-start | bytes 17825792 | tf_op jit(solution)/shard_map/all_gather | solution.py:17
  7.2 2.5 copy-start.13
  9.7 1.5 copy-start.10
  10.4 21.7 %copy-start.9 = (bf16[40,8,32,128]{3,2,1,0:T(8,128)(2,1)}, bf16[40,8,32,128]{3,2,1,0:T(8,128)(2,1)S(1)}, u32[]{:S(2)}) copy-start(bf16[40,8,32,128]{3,2,1,0:T(8,128)(2,1)S(1)} %copy.72) | copy-start | bytes 7864324
  15.9 280.4 %all-gather.7.cloned.1.call-start = ((), (), s32[]{:S(2)}) async-start(), calls=%async_computation.1 | async-start | bytes 17825792 | tf_op jit(solution)/shard_map/all_gather | solution.py:17
  16.3 2.5 copy-start.12
  18.9 4.1 %copy-start.4 = (bf16[40,8,32,128]{3,2,1,0:T(8,128)(2,1)}, bf16[40,8,32,128]{3,2,1,0:T(8,128)(2,1)S(1)}, u32[]{:S(2)}) copy-start(bf16[40,8,32,128]{3,2,1,0:T(8,128)(2,1)S(1)} %copy.70) | copy-start | bytes 7864324
  32.1 3.0 copy-start.7
  130.7 0.7 copy-start.14
  131.3 9.8 %slice-start = ((s8[5242880]{0:T(1024)(128)(4,1)}), s8[4194304]{0:T(1024)(128)(4,1)S(1)}, s32[]{:S(2)}) async-start(s8[5242880]{0:T(1024)(128)(4,1)} %bitcast.68), calls=%async_computation.2 | async-start | bytes 8388608
  131.4 9.8 %slice-start.1 = ((s8[5242880]{0:T(1024)(128)(4,1)}), s8[1048576]{0:T(1024)(128)(4,1)S(1)}, s32[]{:S(2)}) async-start(s8[5242880]{0:T(1024)(128)(4,1)} %bitcast.68), calls=%async_computation.3 | async-start | bytes 2097152
  141.1 3.9 %copy-start = (f32[320,32,128]{2,0,1:T(8,128)}, f32[320,32,128]{2,0,1:T(8,128)S(1)}, u32[]{:S(2)}) copy-start(f32[320,32,128]{2,0,1:T(8,128)S(1)} %get-tuple-element.112) | copy-start | bytes 15728644
  141.2 5.4 %copy-start.5 = (bf16[40,8,32,128]{3,2,1,0:T(8,128)(2,1)S(1)}, bf16[40,8,32,128]{3,2,1,0:T(8,128)(2,1)}, u32[]{:S(2)}) copy-start(bf16[40,8,32,128]{3,2,1,0:T(8,128)(2,1)} %copy-done.4) | copy-start | bytes 7864324
  145.1 1.5 copy-start.1
  166.1 6.3 %copy-start.11 = (bf16[40,8,32,128]{3,2,1,0:T(8,128)(2,1)S(1)}, bf16[40,8,32,128]{3,2,1,0:T(8,128)(2,1)}, u32[]{:S(2)}) copy-start(bf16[40,8,32,128]{3,2,1,0:T(8,128)(2,1)} %copy-done.10) | copy-start | bytes 7864324
  172.4 3.6 %copy-start.8 = (bf16[32,320,320]{2,1,0:T(8,128)(2,1)}, bf16[32,320,320]{2,1,0:T(8,128)(2,1)S(1)}, u32[]{:S(2)}) copy-start(bf16[32,320,320]{2,1,0:T(8,128)(2,1)S(1)} %select_convert_fusion) | copy-start | bytes 19660804
  172.4 3.7 %copy-start.2 = (bf16[320,32,128]{2,0,1:T(8,128)(2,1)S(1)}, bf16[320,32,128]{2,0,1:T(8,128)(2,1)}, u32[]{:S(2)}) copy-start(bf16[320,32,128]{2,0,1:T(8,128)(2,1)} %copy-done.1) | copy-start | bytes 7864324
  181.9 100.1 %copy-start.6 = (bf16[40,8,32,128]{3,2,1,0:T(8,128)(2,1)S(1)}, bf16[40,8,32,128]{3,2,1,0:T(8,128)(2,1)}, u32[]{:S(2)}) copy-start(bf16[40,8,32,128]{3,2,1,0:T(8,128)(2,1)} %copy-done.4) | copy-start | bytes 7864324
  323.6 5.7 %copy-start.3 = (bf16[320,32,128]{2,0,1:T(8,128)(2,1)S(1)}, bf16[320,32,128]{2,0,1:T(8,128)(2,1)}, u32[]{:S(2)}) copy-start(bf16[320,32,128]{2,0,1:T(8,128)(2,1)} %copy-done.1) | copy-start | bytes 7864324
Sparse Core Ops, SparseCore 0:
  16.1 114.3 all-gather.4
  151.4 138.5 all-gather.6
where the time goes:
time: 366 us; the launch traced here: 362 us
  blocking collectives  95.7 us (26%)
  waiting for transfers between devices  90 us (25%)
  matrix products  70.4 us (19%)
  local copies, waits for them, and re-layouts  49.4 us (13%)
  other arithmetic  39.7 us (11%)
  between operations  14.5 us (4%)
    psum x1, blocking collectives, shards(): gain_grad = lax.psum(gain_part, ('dp', 'context'))  95.7 us
    all_gather x2, waiting for transfers between devices, carried_in(): gathered = lax.all_gather(array.astype(jnp.bfloat16), axis)  90 us
    add x15, other arithmetic, add_states(): return earlier + later_one  26.1 us
    unnamed x38, local copies, waits for them, and re-layouts  14.8 us
    dot_general x1, matrix products, shards(): jnp.einsum('lyq,yqd->lyd', local_query_rows, preceding_block, preferred_e...  9.7 us
    dot_general x1, matrix products, shards(): jnp.einsum('hts,thk->shk', d_weights, local_query_rows, preferred_element...  9.63 us
    dot_general x1, matrix products, shards(): jnp.einsum('thk,shk->hts', local_query_rows, local_key_rows, preferred_el...  9.17 us
    convert_element_type x2, local copies, waits for them, and re-layouts, shards(): value_grad.reshape(flat).astype(jnp.bfloat16)  8.36 us
  transfers between devices with their start and end apart: 2, of which 1 were waited for; matrix products, arithmetic and copies ran while one was open for 19% of the time, Pallas kernels for 0%

commit v1 on v0

v1 whole, which is shorter than its diff:
```python
import jax
import jax.numpy as jnp
from jax import lax
from jax.experimental import pallas as pl
from jax.experimental.pallas import tpu as pltpu
from jax.sharding import PartitionSpec as P

HD = 128
EPS = 1e-06
F32 = jnp.float32
BF16 = jnp.bfloat16
MESH = pl.DeviceIdType.MESH


def dot(a, b, ca, cb):
    return lax.dot_general(a, b, (((ca,), (cb,)), ((), ())), preferred_element_type=F32)


def make_kernel(tok, feat, nc, ndp):
    heads = feat // HD
    per = heads // nc
    wid = per * HD

    def kernel(
        q_h, k_h, v_h, g_h, d_h,
        out_h, qg_h, kg_h, vg_h, gg_o,
        q_v, k_v, v_v, d_v, gain, out_v, qg_v, kg_v, vg_v,
        mix, acc, aw, ssq, cdt,
        s1, r1, p1, l1, s2, r2, p2, l2,
        gs, g1, g2s, g2, g3s, g3,
        in_sem, gain_sem, o_sem,
        s1_s, s1_r, p1_s, p1_r, s2_s, s2_r, p2_s, p2_r,
        g1_s, g1_r, g2_s, g2_r, g3_s, g3_r,
    ):
        me = lax.axis_index("context")
        row = lax.axis_index("dp")

        def cols(o):
            return pl.ds(pl.multiple_of(o * wid, wid), wid)

        def hcols(h):
            return pl.ds(pl.multiple_of(h * HD, HD), HD)

        def nxt(i):
            return lax.rem(me + 1 + i, nc)

        def load(src, dst, which, i):
            o = nxt(i)
            return pltpu.make_async_copy(src.at[:, cols(o)], dst.at[:, cols(o)], in_sem.at[which, i])

        def each(n, f):
            def body(i, carry):
                f(i)
                return carry

            lax.fori_loop(0, n, body, 0)

        def start_kv(i):
            load(k_h, k_v, 0, i).start()
            load(v_h, v_v, 1, i).start()

        def start_qd(i):
            load(q_h, q_v, 2, i).start()

        def start_d(i):
            load(d_h, d_v, 3, i).start()

        each(nc, start_kv)
        each(nc, start_qd)
        each(nc, start_d)
        gain_copy = pltpu.make_async_copy(g_h, gain, gain_sem)
        gain_copy.start()

        barrier = pltpu.get_barrier_semaphore()

        def greet_c(i):
            pl.semaphore_signal(barrier, inc=1, device_id={"context": lax.rem(me + 1 + i, nc)}, device_id_type=MESH)

        def greet_d(i):
            pl.semaphore_signal(barrier, inc=1, device_id={"dp": lax.rem(row + 1 + i, ndp)}, device_id_type=MESH)

        each(nc - 1, greet_c)
        each(ndp - 1, greet_d)
        pl.semaphore_wait(barrier, nc - 1 + ndp - 1)

        def ctx_copy(src, dst, ssem, rsem, i):
            to = lax.rem(me + 1 + i, nc)
            return pltpu.make_async_remote_copy(
                src_ref=src, dst_ref=dst.at[me], send_sem=ssem.at[i], recv_sem=rsem.at[i],
                device_id={"context": to}, device_id_type=MESH,
            )

        def dp_copy(src, dst, ssem, rsem, i):
            to = lax.rem(row + 1 + i, ndp)
            return pltpu.make_async_remote_copy(
                src_ref=src, dst_ref=dst.at[row], send_sem=ssem.at[i], recv_sem=rsem.at[i],
                device_id={"dp": to}, device_id_type=MESH,
            )

        def state_of(a, b, o, buf):
            for j in range(per):
                c = hcols(o * per + j)
                buf[o, j] = dot(a[:, c], b[:, c], 0, 0).astype(BF16)

        def step1(i):
            o = nxt(i)
            load(k_h, k_v, 0, i).wait()
            load(v_h, v_v, 1, i).wait()
            state_of(k_v, v_v, o, s1)

        def send1(i):
            ctx_copy(s1.at[nxt(i)], r1, s1_s, s1_r, i).start()

        def one1(i):
            step1(i)
            send1(i)

        each(nc - 1, one1)
        step1(nc - 1)
        r1[me] = s1[me]

        rows_i = lax.broadcasted_iota(jnp.int32, (tok, tok), 0)
        cols_i = lax.broadcasted_iota(jnp.int32, (tok, tok), 1)

        def inner(i):
            o = nxt(i)
            load(q_h, q_v, 2, i).wait()
            for j in range(per):
                h = o * per + j
                c = hcols(h)
                s = dot(q_v[:, c], k_v[:, c], 1, 1)
                a = jnp.where(rows_i >= cols_i, s, 0.0).astype(BF16)
                aw[h] = a
                mix[:, c] = dot(a, v_v[:, c], 1, 0)

        half = nc // 2
        each(half, inner)

        def scan(r, p, backward):
            def rows16(t, carry):
                rr = pl.ds(pl.multiple_of(t * 16, 16), 16)
                run = jnp.zeros((per, 16, HD), F32)
                for c in range(nc):
                    b = nc - 1 - c if backward else c
                    p[b, :, rr, :] = run.astype(BF16)
                    run = run + r[b, :, rr, :].astype(F32)
                return carry

            lax.fori_loop(0, HD // 16, rows16, 0)

        def wait_r1(i):
            ctx_copy(s1.at[nxt(i)], r1, s1_s, s1_r, i).wait_recv()

        each(nc - 1, wait_r1)
        scan(r1, p1, False)

        def back1(i):
            return ctx_copy(p1.at[nxt(i)], l1, p1_s, p1_r, i)

        each(nc - 1, lambda i: back1(i).start())
        l1[me] = p1[me]

        each(nc - half, lambda i: inner(i + half))
        gain_copy.wait()

        ssq[...] = jnp.zeros_like(ssq)
        cdt[...] = jnp.zeros_like(cdt)

        def mixed(i):
            o = nxt(i)
            load(d_h, d_v, 3, i).wait()
            for j in range(per):
                h = o * per + j
                c = hcols(h)
                m = mix[:, c] + dot(q_v[:, c], l1[o, j], 1, 0)
                mix[:, c] = m
                ssq[...] += m * m
                cdt[...] += (gain[:, c] * d_v[:, c].astype(F32)) * m

        mixed(nc - 1)

        def mixed_next(i):
            back1(nc - 2 - i).wait_recv()
            mixed(i)

        each(nc - 1, mixed_next)

        inv = lax.rsqrt(jnp.sum(ssq[...], 1, keepdims=True) / feat + EPS)
        coef = inv * inv * inv * (jnp.sum(cdt[...], 1, keepdims=True) / feat)

        def post(i):
            o = nxt(i)
            for j in range(per):
                h = o * per + j
                c = hcols(h)
                m = mix[:, c]
                dy = d_v[:, c].astype(F32)
                g = gain[:, c]
                n = m * inv
                out_v[:, c] = (n * g).astype(BF16)
                gs[:, c] = jnp.sum((dy * n).reshape(tok // 8, 8, HD), 0)
                d_v[:, c] = (inv * (g * dy) - m * coef).astype(BF16)
            pltpu.make_async_copy(out_v.at[:, cols(o)], out_h.at[:, cols(o)], o_sem.at[0]).start()
            state_of(q_v, d_v, o, s2)

        def gsend(i):
            return ctx_copy(gs.at[:, cols(nxt(i))], g1, g1_s, g1_r, i)

        def send2(i):
            return ctx_copy(s2.at[nxt(i)], r2, s2_s, s2_r, i)

        def one2(i):
            post(i)
            send2(i).start()

        each(nc - 1, one2)
        post(nc - 1)
        each(nc - 1, lambda i: gsend(i).start())
        r2[me] = s2[me]
        g1[me] = gs[:, cols(me)]

        def grads(i):
            o = nxt(i)
            for j in range(per):
                h = o * per + j
                c = hcols(h)
                dm = d_v[:, c]
                s = dot(dm, v_v[:, c], 1, 1)
                dw = jnp.where(rows_i >= cols_i, s, 0.0).astype(BF16)
                qg = dot(dw, k_v[:, c], 1, 0) + dot(dm, l1[o, j], 1, 1)
                qg_v[:, c] = qg.astype(BF16)
                mix[:, c] = dot(dw, q_v[:, c], 0, 0)
                acc[:, c] = dot(aw[h], dm, 0, 0)
            pltpu.make_async_copy(qg_v.at[:, cols(o)], qg_h.at[:, cols(o)], o_sem.at[1]).start()

        each(half, grads)

        each(nc - 1, lambda i: send2(i).wait_recv())
        scan(r2, p2, True)

        def back2(i):
            return ctx_copy(p2.at[nxt(i)], l2, p2_s, p2_r, i)

        each(nc - 1, lambda i: back2(i).start())
        l2[me] = p2[me]

        each(nc - 1, lambda i: gsend(i).wait_recv())
        part = g1[0]
        for c in range(1, nc):
            part = part + g1[c]
        g2s[...] = part
        g2[row] = part
        gdp = lambda i: dp_copy(g2s, g2, g2_s, g2_r, i)
        each(ndp - 1, lambda i: gdp(i).start())

        each(nc - half, lambda i: grads(i + half))

        each(ndp - 1, lambda i: gdp(i).wait_recv())
        total = g2[0]
        for c in range(1, ndp):
            total = total + g2[c]
        total = jnp.broadcast_to(jnp.sum(total, 0, keepdims=True), (8, wid))
        g3s[...] = total
        g3[me] = total
        gback = lambda i: ctx_copy(g3s, g3, g3_s, g3_r, i)
        each(nc - 1, lambda i: gback(i).start())

        def final(i):
            o = nxt(i)
            for j in range(per):
                h = o * per + j
                c = hcols(h)
                lb = l2[o, j]
                kg_v[:, c] = (mix[:, c] + dot(v_v[:, c], lb, 1, 1)).astype(BF16)
                vg_v[:, c] = (acc[:, c] + dot(k_v[:, c], lb, 1, 0)).astype(BF16)
            pltpu.make_async_copy(kg_v.at[:, cols(o)], kg_h.at[:, cols(o)], o_sem.at[2]).start()
            pltpu.make_async_copy(vg_v.at[:, cols(o)], vg_h.at[:, cols(o)], o_sem.at[3]).start()

        final(nc - 1)

        def final_next(i):
            back2(nc - 2 - i).wait_recv()
            final(i)

        each(nc - 1, final_next)

        each(nc - 1, lambda i: gback(i).wait_recv())
        for c in range(nc):
            gg_o[:, c * wid : (c + 1) * wid] = g3[c]

        def drain(i):
            ctx_copy(s1.at[nxt(i)], r1, s1_s, s1_r, i).wait_send()
            back1(i).wait_send()
            send2(i).wait_send()
            back2(i).wait_send()
            gsend(i).wait_send()
            gback(i).wait_send()

        each(nc - 1, drain)
        each(ndp - 1, lambda i: gdp(i).wait_send())
        pltpu.make_async_copy(out_v, out_h, o_sem.at[0]).wait()
        pltpu.make_async_copy(qg_v, qg_h, o_sem.at[1]).wait()
        pltpu.make_async_copy(kg_v, kg_h, o_sem.at[2]).wait()
        pltpu.make_async_copy(vg_v, vg_h, o_sem.at[3]).wait()

    big = jax.ShapeDtypeStruct((tok, feat), BF16)
    bufb = pltpu.VMEM((tok, feat), BF16)
    buff = pltpu.VMEM((tok, feat), F32)
    state = pltpu.VMEM((nc, per, HD, HD), BF16)
    csem = pltpu.SemaphoreType.DMA((nc - 1,))
    dsem = pltpu.SemaphoreType.DMA((ndp - 1,))
    anyspec = pl.BlockSpec(memory_space=pl.ANY)
    return pl.pallas_call(
        kernel,
        out_shape=(big, big, big, big, jax.ShapeDtypeStruct((8, feat), F32)),
        in_specs=[anyspec] * 5,
        out_specs=[anyspec] * 4 + [pl.BlockSpec(memory_space=pltpu.VMEM)],
        scratch_shapes=[
            bufb, bufb, bufb, bufb, pltpu.VMEM((1, feat), F32), bufb, bufb, bufb, bufb,
            buff, buff, pltpu.VMEM((heads, tok, tok), BF16),
            pltpu.VMEM((tok, HD), F32), pltpu.VMEM((tok, HD), F32),
            state, state, state, state, state, state, state, state,
            pltpu.VMEM((8, feat), F32), pltpu.VMEM((nc, 8, wid), F32),
            pltpu.VMEM((8, wid), F32), pltpu.VMEM((ndp, 8, wid), F32),
            pltpu.VMEM((8, wid), F32), pltpu.VMEM((nc, 8, wid), F32),
            pltpu.SemaphoreType.DMA((4, nc)), pltpu.SemaphoreType.DMA, pltpu.SemaphoreType.DMA((4,)),
            csem, csem, csem, csem, csem, csem, csem, csem,
            csem, csem, dsem, dsem, csem, csem,
        ],
        compiler_params=pltpu.CompilerParams(
            collective_id=0, has_side_effects=True, vmem_limit_bytes=67043328
        ),
        name="layer",
    )


def solution(mesh):
    nc, ndp = mesh.shape["context"], mesh.shape["dp"]

    def shards(queries, keys, values, gain, out_grad):
        tok, feat = queries.shape[1:]
        call = make_kernel(tok, feat, nc, ndp)
        out, qg, kg, vg, gg = call(queries[0], keys[0], values[0], gain[None], out_grad[0])
        return out[None], qg[None], kg[None], vg[None], gg[0]

    spec = P("dp", "context", None)
    return jax.shard_map(
        shards, mesh=mesh, in_specs=(spec, spec, spec, P(), spec),
        out_specs=(spec, spec, spec, spec, P()), check_vma=False,
    )
```

time: 366 us -> 97.3 us (0.27); the launches traced: 362 us -> 97.1 us
  blocking collectives: 95.7 us -> 0 us
  waiting for transfers between devices: 90 us -> 0 us
  Pallas kernels: 0 us -> 84.4 us
  matrix products: 70.4 us -> 0 us
  other arithmetic: 39.7 us -> 0 us
  local copies, waits for them, and re-layouts: 49.4 us -> 12.1 us
  between operations: 14.5 us -> 0.65 us
    psum x1 -> x0, blocking collectives: 95.7 us -> none  [shards(): gain_grad = lax.psum(gain_part, ('dp', 'context'))]
    all_gather x2 -> x0, waiting for transfers between devices: 90 us -> none  [carried_in(): gathered = lax.all_gather(array.astype(jnp.bfloat16), axis)]
    pallas_call x0 -> x1, Pallas kernels: none -> 84.4 us  [shards(): call(queries[0], keys[0], values[0], gain[None], out_grad[0])]
    dot_general x12 -> x0, matrix products: 70.4 us -> none  [the longest x1 9.7 us: shards(): jnp.einsum('lyq,yqd->lyd', local_query_rows, preceding_block, preferred_e...]
    add x15 -> x0, other arithmetic: 26.1 us -> none  [add_states(): return earlier + later_one]
    convert_element_type x7 -> x0, local copies, waits for them, and re-layouts: 19.2 us -> none  [the longest x2 8.36 us: shards(): value_grad.reshape(flat).astype(jnp.bfloat16)]
    convert_element_type x2 -> x0, other arithmetic: 8.57 us -> none  [the longest x1 4.73 us: shards(): output = (normed * gain).astype(jnp.bfloat16)]
    add x1 -> x0, local copies, waits for them, and re-layouts: 7.89 us -> none  [shards(): mixed_out + jnp.einsum('lyq,yqd->lyd', local_query_rows, preceding_block,...]
  transfers between devices with their start and end apart: 2 -> 0, of which waited for: 1 -> 0; matrix products, arithmetic and copies ran while one was open for 19% -> 0% of each run, Pallas kernels for 0% -> 0%
where the time goes in v1:
time: 97.3 us; the launch traced here: 97.1 us
  Pallas kernels  84.4 us (87%)
  local copies, waits for them, and re-layouts  12.1 us (12%)
    pallas_call x1, Pallas kernels, shards(): call(queries[0], keys[0], values[0], gain[None], out_grad[0])  84.4 us
    unnamed x10, local copies, waits for them, and re-layouts  10.5 us

profile of v1, /device:TPU:1, one launch (start us, length us, event | category | flops | bytes accessed | tf_op | source)
XLA Modules:
  0.0 97.1 jit_solution(16479125541694996385)
XLA Ops:
  0.6 84.4 %layer.1 = (bf16[320,4096]{1,0:T(8,128)(2,1)}, bf16[320,4096]{1,0:T(8,128)(2,1)}, bf16[320,4096]{1,0:T(8,128)(2,1)}, bf16[320,4096]{1,0:T(8,128)(2,1)}, f32[8,4096]{1,0:T(8,128)}) custom-call(bf16[320,4096]{1,0:T(8,128)(2,1)} %bitcast.10, bf16[320,4096]{1,0:T(8,128)(2,1)} %bitcast.11, bf16[320,4096]{1,0:T(8,128)(2,1)} %bitcast.12, f32[1,4096]{1,0:T(1,128)} %bitcast.18, ...), custom_call_target="tpu_custom_call" | custom-call | tf_op jit(solution)/shard_map/layer/pallas_call | solution.py:343
  85.0 1.5 %slice.3 = f32[1,4096]{1,0:T(1,128)} slice(f32[8,4096]{1,0:T(8,128)} %get-tuple-element.14), slice={[0:1], [0:4096]} | slice | bytes 32768 | tf_op jit(solution)/shard_map/slice | solution.py:344
  86.6 0.0 copy-start.2
  86.6 3.7 %copy.14 = bf16[1,320,4096]{2,1,0:T(8,128)(2,1)} copy(bf16[1,320,4096]{2,1,0:T(8,128)(2,1)} %bitcast.17) | data formatting | bytes 5242880
  90.2 0.0 copy-done.2
  90.2 0.0 copy-start.1
  90.2 1.5 %copy.15 = bf16[1,320,4096]{2,1,0:T(8,128)(2,1)} copy(bf16[1,320,4096]{2,1,0:T(8,128)(2,1)S(1)} %bitcast.16) | data formatting | bytes 5242880
  91.7 1.2 %copy-done.1 = bf16[320,4096]{1,0:T(8,128)(2,1)S(1)} copy-done((bf16[320,4096]{1,0:T(8,128)(2,1)S(1)}, bf16[320,4096]{1,0:T(8,128)(2,1)}, u32[]{:S(2)}) %copy-start.1) | copy-done | bytes 2621464
  92.9 0.0 copy-start
  92.9 1.5 %copy.16 = bf16[1,320,4096]{2,1,0:T(8,128)(2,1)} copy(bf16[1,320,4096]{2,1,0:T(8,128)(2,1)S(1)} %bitcast.15) | data formatting | bytes 5242880
  94.4 1.2 %copy-done = bf16[320,4096]{1,0:T(8,128)(2,1)S(1)} copy-done((bf16[320,4096]{1,0:T(8,128)(2,1)S(1)}, bf16[320,4096]{1,0:T(8,128)(2,1)}, u32[]{:S(2)}) %copy-start) | copy-done | bytes 2621464
  95.6 1.5 %copy.17 = bf16[1,320,4096]{2,1,0:T(8,128)(2,1)} copy(bf16[1,320,4096]{2,1,0:T(8,128)(2,1)S(1)} %bitcast.14) | data formatting | bytes 5242880
Async XLA Ops:
  86.6 3.7 %copy-start.2 = (bf16[320,4096]{1,0:T(8,128)(2,1)S(1)}, bf16[320,4096]{1,0:T(8,128)(2,1)}, u32[]{:S(2)}) copy-start(bf16[320,4096]{1,0:T(8,128)(2,1)} %get-tuple-element.11) | copy-start | bytes 7864324
  90.2 2.7 %copy-start.1 = (bf16[320,4096]{1,0:T(8,128)(2,1)S(1)}, bf16[320,4096]{1,0:T(8,128)(2,1)}, u32[]{:S(2)}) copy-start(bf16[320,4096]{1,0:T(8,128)(2,1)} %get-tuple-element.12) | copy-start | bytes 7864324
  92.9 2.7 %copy-start = (bf16[320,4096]{1,0:T(8,128)(2,1)S(1)}, bf16[320,4096]{1,0:T(8,128)(2,1)}, u32[]{:S(2)}) copy-start(bf16[320,4096]{1,0:T(8,128)(2,1)} %get-tuple-element.13) | copy-start | bytes 7864324

commit v2 on v1

v2 whole, which is shorter than its diff:
```python
import jax
import jax.numpy as jnp
from jax import lax
from jax.experimental import pallas as pl
from jax.experimental.pallas import tpu as pltpu
from jax.sharding import PartitionSpec as P

HD = 128
EPS = 1e-06
NY = 4
F32 = jnp.float32
BF16 = jnp.bfloat16
MESH = pl.DeviceIdType.MESH

FAR_FIRST = sorted(
    ((dz, dy) for dz in range(4) for dy in range(4) if dz or dy),
    key=lambda d: -(min(d[0], 4 - d[0]) + min(d[1], 4 - d[1])),
)


def dot(a, b, ca, cb):
    return lax.dot_general(a, b, (((ca,), (cb,)), ((), ())), preferred_element_type=F32)


def pick(i, values):
    if isinstance(i, int):
        return values[i]
    out = 0
    for k, v in enumerate(values):
        if v:
            out = out + jnp.where(i == k, v, 0)
    return out


def each(n, f, start=0, unroll=1):
    def body(i, carry):
        f(i)
        return carry

    lax.fori_loop(start, n, body, 0, unroll=unroll)


def hcols(h):
    return pl.ds(pl.multiple_of(h * HD, HD), HD)


def make_layer(tok, feat, nc, ndp):
    heads = feat // HD
    per = heads // nc
    wid = per * HD
    nz = nc // NY
    steps = FAR_FIRST + [(0, 0)]

    def kernel(
        q_h, k_h, v_h, g_h, d_h,
        out_v, qg_v, mix, acc, k_v, v_v, l2, gg,
        q_v, d_v, gain, aw, ssq, cdt,
        s1, r1, p1, l1, s2, r2, p2,
        gs, g1, g2s, g2, g3s, g3,
        in_sem, gain_sem,
        s1_s, s1_r, p1_s, p1_r, s2_s, s2_r, p2_s, p2_r,
        g1_s, g1_r, g2_s, g2_r, g3_s, g3_r,
    ):
        me = lax.axis_index("context")
        row = lax.axis_index("dp")
        mz, my = me // NY, lax.rem(me, NY)
        others = range(nc - 1)

        def cols(o):
            return pl.ds(pl.multiple_of(o * wid, wid), wid)

        def dest(i):
            dz, dy = pick(i, [s[0] for s in steps]), pick(i, [s[1] for s in steps])
            return lax.rem(mz + dz, nz) * NY + lax.rem(my + dy, NY)

        def source(i):
            dz, dy = pick(i, [(nz - s[0]) % nz for s in steps]), pick(i, [(NY - s[1]) % NY for s in steps])
            return lax.rem(mz + dz, nz) * NY + lax.rem(my + dy, NY)

        def load(src, dst, which, i):
            o = dest(i)
            return pltpu.make_async_copy(src.at[:, cols(o)], dst.at[:, cols(o)], in_sem.at[which, i])

        def start_kv(i):
            load(k_h, k_v, 0, i).start()
            load(v_h, v_v, 1, i).start()

        each(nc, start_kv)
        each(nc, lambda i: load(q_h, q_v, 2, i).start())
        each(nc, lambda i: load(d_h, d_v, 3, i).start())
        gain_copy = pltpu.make_async_copy(g_h, gain, gain_sem)
        gain_copy.start()

        barrier = pltpu.get_barrier_semaphore()

        def greet_c(i):
            pl.semaphore_signal(barrier, inc=1, device_id={"context": lax.rem(me + 1 + i, nc)}, device_id_type=MESH)

        def greet_d(i):
            pl.semaphore_signal(barrier, inc=1, device_id={"dp": lax.rem(row + 1 + i, ndp)}, device_id_type=MESH)

        each(nc - 1, greet_c)
        each(ndp - 1, greet_d)
        pl.semaphore_wait(barrier, nc - 1 + ndp - 1)

        def head_copy(src, dst, ssem, rsem, i, j):
            to = dest(i)
            return pltpu.make_async_remote_copy(
                src_ref=src.at[to, j], dst_ref=dst.at[me, j], send_sem=ssem.at[j, i], recv_sem=rsem.at[j, i],
                device_id={"context": to}, device_id_type=MESH,
            )

        def ctx_copy(src, dst, ssem, rsem, i):
            return pltpu.make_async_remote_copy(
                src_ref=src, dst_ref=dst.at[me], send_sem=ssem.at[i], recv_sem=rsem.at[i],
                device_id={"context": dest(i)}, device_id_type=MESH,
            )

        def dp_copy(src, dst, ssem, rsem, i):
            return pltpu.make_async_remote_copy(
                src_ref=src, dst_ref=dst.at[row], send_sem=ssem.at[i], recv_sem=rsem.at[i],
                device_id={"dp": lax.rem(row + 1 + i, ndp)}, device_id_type=MESH,
            )

        send1 = lambda i, j: head_copy(s1, r1, s1_s, s1_r, i, j)
        back1 = lambda i, j: head_copy(p1, l1, p1_s, p1_r, i, j)
        send2 = lambda i, j: head_copy(s2, r2, s2_s, s2_r, i, j)
        back2 = lambda i, j: head_copy(p2, l2, p2_s, p2_r, i, j)

        def state_of(a, b, o, j, buf):
            c = hcols(o * per + j)
            buf[o, j] = dot(a[:, c], b[:, c], 0, 0).astype(BF16)

        for j in range(per):
            def state1(i, j=j):
                if j == 0:
                    load(k_h, k_v, 0, i).wait()
                    load(v_h, v_v, 1, i).wait()
                state_of(k_v, v_v, dest(i), j, s1)

            def one1(i, j=j):
                state1(i)
                send1(i, j).start()

            each(nc - 1, one1, unroll=3)
            state1(nc - 1)
            r1[me, j] = s1[me, j]

        rows_i = lax.broadcasted_iota(jnp.int32, (tok, tok), 0)
        cols_i = lax.broadcasted_iota(jnp.int32, (tok, tok), 1)

        def inner(i):
            o = dest(i)
            load(q_h, q_v, 2, i).wait()
            for j in range(per):
                h = o * per + j
                c = hcols(h)
                s = dot(q_v[:, c], k_v[:, c], 1, 1)
                a = jnp.where(rows_i >= cols_i, s, 0.0).astype(BF16)
                aw[h] = a
                mix[:, c] = dot(a, v_v[:, c], 1, 0)

        def scan(r, p, j, backward):
            def rows16(t):
                rr = pl.ds(pl.multiple_of(t * 16, 16), 16)
                run = jnp.zeros((16, HD), F32)
                for c in range(nc):
                    b = nc - 1 - c if backward else c
                    p[b, j, rr, :] = run.astype(BF16)
                    run = run + r[b, j, rr, :].astype(F32)

            each(HD // 16, rows16, unroll=2)

        def turn(send, back, r, p, l, j, backward):
            for i in others:
                send(i, j).wait_recv()
            scan(r, p, j, backward)
            for i in others:
                back(i, j).start()
            l[me, j] = p[me, j]

        n1 = 11
        each(n1, inner)
        turn(send1, back1, r1, p1, l1, 0, False)
        each(nc, inner, n1)
        turn(send1, back1, r1, p1, l1, 1, False)
        gain_copy.wait()
        each(nc, lambda i: load(d_h, d_v, 3, i).wait())

        ssq[...] = jnp.zeros_like(ssq)
        cdt[...] = jnp.zeros_like(cdt)

        def mixed(o, j):
            c = hcols(o * per + j)
            m = mix[:, c] + dot(q_v[:, c], l1[o, j], 1, 0)
            mix[:, c] = m
            ssq[...] += m * m
            cdt[...] += (gain[:, c] * d_v[:, c].astype(F32)) * m

        for j in range(per):
            mixed(me, j)

            def mixed_next(i, j=j):
                back1(i, j).wait_recv()
                mixed(source(i), j)

            each(nc - 1, mixed_next)

        inv = lax.rsqrt(jnp.sum(ssq[...], 1, keepdims=True) / feat + EPS)
        coef = inv * inv * inv * (jnp.sum(cdt[...], 1, keepdims=True) / feat)

        def post(i):
            o = dest(i)
            for j in range(per):
                c = hcols(o * per + j)
                m = mix[:, c]
                dy = d_v[:, c].astype(F32)
                g = gain[:, c]
                n = m * inv
                out_v[:, c] = (n * g).astype(BF16)
                gs[:, c] = jnp.sum((dy * n).reshape(tok // 8, 8, HD), 0)
                d_v[:, c] = (inv * (g * dy) - m * coef).astype(BF16)
            state_of(q_v, d_v, o, 0, s2)

        gsend = lambda i: ctx_copy(gs.at[:, cols(dest(i))], g1, g1_s, g1_r, i)

        def one2(i):
            post(i)
            send2(i, 0).start()

        each(nc - 1, one2)
        post(nc - 1)
        for i in others:
            gsend(i).start()
        r2[me, 0] = s2[me, 0]
        g1[me] = gs[:, cols(me)]

        for j in range(1, per):
            def two2(i, j=j):
                state_of(q_v, d_v, dest(i), j, s2)
                send2(i, j).start()

            each(nc - 1, two2, unroll=3)
            state_of(q_v, d_v, me, j, s2)
            r2[me, j] = s2[me, j]

        def grads(i):
            o = dest(i)
            for j in range(per):
                h = o * per + j
                c = hcols(h)
                dm = d_v[:, c]
                s = dot(dm, v_v[:, c], 1, 1)
                dw = jnp.where(rows_i >= cols_i, s, 0.0).astype(BF16)
                qg = dot(dw, k_v[:, c], 1, 0) + dot(dm, l1[o, j], 1, 1)
                qg_v[:, c] = qg.astype(BF16)
                mix[:, c] = dot(dw, q_v[:, c], 0, 0)
                acc[:, c] = dot(aw[h], dm, 0, 0)

        m1, m2 = 3, 8
        each(m1, grads)
        turn(send2, back2, r2, p2, l2, 0, True)

        for i in others:
            gsend(i).wait_recv()
        part = g1[0]
        for c in range(1, nc):
            part = part + g1[c]
        g2s[...] = part
        g2[row] = part
        gdp = lambda i: dp_copy(g2s, g2, g2_s, g2_r, i)
        for i in range(ndp - 1):
            gdp(i).start()

        each(m2, grads, m1)

        for i in range(ndp - 1):
            gdp(i).wait_recv()
        total = g2[0]
        for c in range(1, ndp):
            total = total + g2[c]
        total = jnp.broadcast_to(jnp.sum(total, 0, keepdims=True), (8, wid))
        g3s[...] = total
        g3[me] = total
        gback = lambda i: ctx_copy(g3s, g3, g3_s, g3_r, i)
        for i in others:
            gback(i).start()

        turn(send2, back2, r2, p2, l2, 1, True)
        each(nc, grads, m2)

        for i in others:
            gback(i).wait_recv()
        for c in range(nc):
            gg[:, c * wid : (c + 1) * wid] = g3[c]

        for i in others:
            for j in range(per):
                send1(i, j).wait_send()
                back1(i, j).wait_send()
                send2(i, j).wait_send()
                back2(i, j).wait_send()
            gsend(i).wait_send()
            gback(i).wait_send()
        for i in range(ndp - 1):
            gdp(i).wait_send()
        for j in range(per):
            for i in others:
                back2(i, j).wait_recv()

    bufb = pltpu.VMEM((tok, feat), BF16)
    buff = pltpu.VMEM((tok, feat), F32)
    state = pltpu.VMEM((nc, per, HD, HD), BF16)
    hsem = pltpu.SemaphoreType.DMA((per, nc - 1))
    csem = pltpu.SemaphoreType.DMA((nc - 1,))
    dsem = pltpu.SemaphoreType.DMA((ndp - 1,))
    part = pltpu.VMEM((8, wid), F32)
    return pl.pallas_call(
        kernel,
        out_shape=(bufb, bufb, buff, buff, bufb, bufb, state, pltpu.VMEM((8, feat), F32)),
        in_specs=[pl.BlockSpec(memory_space=pltpu.MemorySpace.HBM)] * 5,
        out_specs=[pl.BlockSpec(memory_space=pltpu.VMEM)] * 8,
        scratch_shapes=[
            bufb, bufb, pltpu.VMEM((1, feat), F32), pltpu.VMEM((heads, tok, tok), BF16),
            pltpu.VMEM((tok, HD), F32), pltpu.VMEM((tok, HD), F32),
            state, state, state, state, state, state, state,
            pltpu.VMEM((8, feat), F32), pltpu.VMEM((nc, 8, wid), F32),
            part, pltpu.VMEM((ndp, 8, wid), F32), part, pltpu.VMEM((nc, 8, wid), F32),
            pltpu.SemaphoreType.DMA((4, nc)), pltpu.SemaphoreType.DMA,
            hsem, hsem, hsem, hsem, hsem, hsem, hsem, hsem,
            csem, csem, dsem, dsem, csem, csem,
        ],
        compiler_params=pltpu.CompilerParams(
            collective_id=0, has_side_effects=True, vmem_limit_bytes=32 * 2**20
        ),
        name="layer",
    )


def make_finish(tok, feat, nc):
    per = feat // HD // nc
    wid = per * HD

    def kernel(out_v, qg_v, mix, acc, k_v, v_v, l2, gg, out_h, qg_h, kg_h, vg_h, gg_o, kg_v, vg_v, sem):
        whole = [
            pltpu.make_async_copy(out_v, out_h, sem.at[0]),
            pltpu.make_async_copy(qg_v, qg_h, sem.at[1]),
            pltpu.make_async_copy(kg_v, kg_h, sem.at[2]),
            pltpu.make_async_copy(vg_v, vg_h, sem.at[3]),
        ]
        whole[0].start()
        whole[1].start()
        gg_o[...] = gg[0:1, :]

        def final(o):
            cc = pl.ds(pl.multiple_of(o * wid, wid), wid)
            for j in range(per):
                c = hcols(o * per + j)
                lb = l2[o, j]
                kg_v[:, c] = (mix[:, c] + dot(v_v[:, c], lb, 1, 1)).astype(BF16)
                vg_v[:, c] = (acc[:, c] + dot(k_v[:, c], lb, 1, 0)).astype(BF16)
            pltpu.make_async_copy(kg_v.at[:, cc], kg_h.at[:, cc], sem.at[2]).start()
            pltpu.make_async_copy(vg_v.at[:, cc], vg_h.at[:, cc], sem.at[3]).start()

        each(nc, final)
        for w in whole:
            w.wait()

    big = jax.ShapeDtypeStruct((tok, feat), BF16)
    bufb = pltpu.VMEM((tok, feat), BF16)
    vm = pl.BlockSpec(memory_space=pltpu.VMEM)
    return pl.pallas_call(
        kernel,
        out_shape=(big, big, big, big, jax.ShapeDtypeStruct((1, feat), F32)),
        in_specs=[vm] * 8,
        out_specs=[pl.BlockSpec(memory_space=pltpu.MemorySpace.HBM)] * 4 + [vm],
        scratch_shapes=[bufb, bufb, pltpu.SemaphoreType.DMA((4,))],
        compiler_params=pltpu.CompilerParams(vmem_limit_bytes=12 * 2**20),
        name="finish",
    )


def solution(mesh):
    nc, ndp = mesh.shape["context"], mesh.shape["dp"]

    def shards(queries, keys, values, gain, out_grad):
        tok, feat = queries.shape[1:]
        held = make_layer(tok, feat, nc, ndp)(queries[0], keys[0], values[0], gain[None], out_grad[0])
        out, qg, kg, vg, gg = make_finish(tok, feat, nc)(*held)
        return out[None], qg[None], kg[None], vg[None], gg[0]

    spec = P("dp", "context", None)
    return jax.shard_map(
        shards, mesh=mesh, in_specs=(spec, spec, spec, P(), spec),
        out_specs=(spec, spec, spec, spec, P()), check_vma=False,
    )
```

time: 97.3 us -> 83.3 us (0.86)
  the two profiles are of different devices: /device:TPU:1 before, /device:TPU:8 now
where the time goes in v2:
time: 83.3 us; the launch traced here: 83.1 us
  Pallas kernels  81.8 us (98%)
    pallas_call x1, Pallas kernels, shards(): make_layer(tok, feat, nc, ndp)  76.3 us
    pallas_call x1, Pallas kernels, shards(): out, qg, kg, vg, gg = make_finish(tok, feat, nc)(*held)  5.46 us

profile of v2, /device:TPU:8, one launch (start us, length us, event | category | flops | bytes accessed | tf_op | source)
XLA Modules:
  0.0 83.1 jit_solution(15912296327709445973)
XLA Ops:
  0.6 0.0 copy-start
  0.6 0.7 copy-done
  1.4 76.3 %layer.1 = (bf16[320,4096]{1,0:T(8,128)(2,1)S(1)}, bf16[320,4096]{1,0:T(8,128)(2,1)S(1)}, f32[320,4096]{1,0:T(8,128)S(1)}, f32[320,4096]{1,0:T(8,128)S(1)}, bf16...) custom-call(bf16[320,4096]{1,0:T(8,128)(2,1)} %bitcast.11, ...), custom_call_target="tpu_custom_call" | custom-call | tf_op jit(solution)/shard_map/layer/pallas_call | solution.py:388
  77.7 5.5 %finish.1 = (bf16[320,4096]{1,0:T(8,128)(2,1)}, bf16[320,4096]{1,0:T(8,128)(2,1)}, bf16[320,4096]{1,0:T(8,128)(2,1)}, bf16[320,4096]{1,0:T(8,128)(2,1)}, f32[1,4096]{1,0:T(1,128)}) custom-call(bf16[320,4096]{1,0:T(8,128)(2,1)S(1)} %get-tuple-element.18.out_v, bf16[320,4096]{1,0:T(8,128)(2,1)S(1)} %get-tuple-element.19.qg_v, ...), custom_call_target="tpu_custom_call" | custom-call | tf_op jit(solution)/shard_map/finish/pallas_call | solution.py:389
Async XLA Ops:
  0.6 0.7 copy-start

commit v3 on v2

v3 whole, which is shorter than its diff:
```python
import jax
import jax.numpy as jnp
from jax import lax
from jax.experimental import pallas as pl
from jax.experimental.pallas import tpu as pltpu
from jax.sharding import PartitionSpec as P

HD = 128
EPS = 1e-06
NY = 4
F32 = jnp.float32
BF16 = jnp.bfloat16
MESH = pl.DeviceIdType.MESH

FAR_FIRST = sorted(
    ((dz, dy) for dz in range(4) for dy in range(4) if dz or dy),
    key=lambda d: -(min(d[0], 4 - d[0]) + min(d[1], 4 - d[1])),
)


def dot(a, b, ca, cb):
    return lax.dot_general(a, b, (((ca,), (cb,)), ((), ())), preferred_element_type=F32)


def pick(i, values):
    if isinstance(i, int):
        return values[i]
    out = 0
    for k, v in enumerate(values):
        if v:
            out = out + jnp.where(i == k, v, 0)
    return out


def each(n, f, start=0, unroll=1):
    def body(i, carry):
        f(i)
        return carry

    lax.fori_loop(start, n, body, 0, unroll=unroll)


def hcols(h):
    return pl.ds(pl.multiple_of(h * HD, HD), HD)


def make_layer(tok, feat, nc, ndp):
    heads = feat // HD
    per = heads // nc
    wid = per * HD
    nz = nc // NY
    top = min(256, tok)
    low = tok - top
    nload = 8
    lw = feat // nload
    steps = FAR_FIRST + [(0, 0)]

    def kernel(
        q_h, k_h, v_h, g_h, d_h,
        out_v, qg_v, mix, acc, k_v, v_v, l2, gg,
        q_v, d_v, gain, aw0, aw1, ssq, cdt,
        s1, r1, p1, l1, s2, r2, p2,
        gs, g1, g2s, g2, g3s, g3,
        kv_sem, q_sem, d_sem, gain_sem,
        s1_s, s1_r, p1_s, p1_ra, p1_rb, s2_s, s2_r, p2_s, p2_r,
        g1_s, g1_r, g2_s, g2_r, g3_s, g3_r,
    ):
        me = lax.axis_index("context")
        row = lax.axis_index("dp")
        mz, my = me // NY, lax.rem(me, NY)
        others = range(nc - 1)

        def cols(o):
            return pl.ds(pl.multiple_of(o * wid, wid), wid)

        def dest(i):
            dz, dy = pick(i, [s[0] for s in steps]), pick(i, [s[1] for s in steps])
            return lax.rem(mz + dz, nz) * NY + lax.rem(my + dy, NY)

        def source(i):
            dz, dy = pick(i, [(nz - s[0]) % nz for s in steps]), pick(i, [(NY - s[1]) % NY for s in steps])
            return lax.rem(mz + dz, nz) * NY + lax.rem(my + dy, NY)

        barrier = pltpu.get_barrier_semaphore()
        for i in others:
            pl.semaphore_signal(barrier, inc=1, device_id={"context": dest(i)}, device_id_type=MESH)
        for i in range(ndp - 1):
            pl.semaphore_signal(barrier, inc=1, device_id={"dp": lax.rem(row + 1 + i, ndp)}, device_id_type=MESH)

        def kv_load(src, dst, which, i):
            c = slice(i * lw, (i + 1) * lw)
            return pltpu.make_async_copy(src.at[:, c], dst.at[:, c], kv_sem.at[which, i])

        for i in range(nload):
            kv_load(k_h, k_v, 0, i).start()
            kv_load(v_h, v_v, 1, i).start()
        q_copy = pltpu.make_async_copy(q_h, q_v, q_sem)
        d_copy = pltpu.make_async_copy(d_h, d_v, d_sem)
        gain_copy = pltpu.make_async_copy(g_h, gain, gain_sem)
        q_copy.start()
        d_copy.start()
        gain_copy.start()

        def pair_state(a, b, o, buf):
            c = cols(o)
            s = dot(a[:, c], b[:, c], 0, 0)
            for j in range(per):
                buf[o, j] = s[j * HD : (j + 1) * HD, j * HD : (j + 1) * HD].astype(BF16)

        def clear(i):
            for j in range(per):
                for k in range(per):
                    if j != k:
                        z = jnp.zeros((HD, HD), BF16)
                        l1[i, j * HD : (j + 1) * HD, k * HD : (k + 1) * HD] = z
                        l2[i, j * HD : (j + 1) * HD, k * HD : (k + 1) * HD] = z

        each(nc, clear)

        for i in range(nload):
            kv_load(k_h, k_v, 0, i).wait()
            kv_load(v_h, v_v, 1, i).wait()
            for o in range(i * nc // nload, (i + 1) * nc // nload):
                pair_state(k_v, v_v, o, s1)

        pl.semaphore_wait(barrier, nc - 1 + ndp - 1)

        def ctx_copy(src, dst, ssem, rsem, i):
            return pltpu.make_async_remote_copy(
                src_ref=src, dst_ref=dst, send_sem=ssem, recv_sem=rsem,
                device_id={"context": dest(i)}, device_id_type=MESH,
            )

        def out_copy(src, dst, ssem, rsem, i, j):
            return ctx_copy(src.at[dest(i), j], dst.at[me, j], ssem, rsem.at[j], i)

        def back_copy(src, dst, ssem, rsem, i, j):
            place = dst.at[me, j * HD : (j + 1) * HD, j * HD : (j + 1) * HD]
            return ctx_copy(src.at[dest(i), j], place, ssem, rsem, i)

        def take(src, dst, sem):
            pltpu.make_async_copy(src, dst, sem).wait()

        def own_state(p, l, j):
            l[me, j * HD : (j + 1) * HD, j * HD : (j + 1) * HD] = p[me, j]

        def scan(r, p, j, backward):
            def rows32(t):
                rr = pl.ds(pl.multiple_of(t * 32, 32), 32)
                run = jnp.zeros((32, HD), F32)
                for c in range(nc):
                    b = nc - 1 - c if backward else c
                    p[b, j, rr, :] = run.astype(BF16)
                    run = run + r[b, j, rr, :].astype(F32)

            each(HD // 32, rows32, unroll=2)

        def back1(i, j):
            return back_copy(p1, l1, p1_s, p1_ra if j == 0 else p1_rb.at[j - 1, i], i, j)

        def back2(i, j):
            return back_copy(p2, l2, p2_s, p2_r, i, j)

        def turn(s, r, rsem, back, p, l, j, backward):
            take(s.at[0 : nc - 1, j], r.at[0 : nc - 1, j], rsem.at[j])
            scan(r, p, j, backward)
            for i in others:
                back(i, j).start()
            own_state(p, l, j)

        for j in range(per):
            for i in others:
                out_copy(s1, r1, s1_s, s1_r, i, j).start()
            r1[me, j] = s1[me, j]

        keep0 = lax.broadcasted_iota(jnp.int32, (top, top), 0) >= lax.broadcasted_iota(jnp.int32, (top, top), 1)
        keep1 = lax.broadcasted_iota(jnp.int32, (low, tok), 0) + top >= lax.broadcasted_iota(jnp.int32, (low, tok), 1)

        def weights(a, b):
            w0 = jnp.where(keep0, dot(a[:top], b[:top], 1, 1), 0.0).astype(BF16)
            w1 = jnp.where(keep1, dot(a[top:], b, 1, 1), 0.0).astype(BF16)
            return w0, w1

        def inner(o):
            for j in range(per):
                h = o * per + j
                c = hcols(h)
                v = v_v[:, c]
                w0, w1 = weights(q_v[:, c], k_v[:, c])
                aw0[h] = w0
                aw1[h] = w1
                mix[:top, c] = dot(w0, v[:top], 1, 0)
                mix[top:, c] = dot(w1, v, 1, 0)

        q_copy.wait()
        n1 = 13
        each(n1, inner)
        turn(s1, r1, s1_r, back1, p1, l1, 0, False)
        each(nc, inner, n1)
        for j in range(1, per):
            turn(s1, r1, s1_r, back1, p1, l1, j, False)
        gain_copy.wait()
        d_copy.wait()

        ssq[...] = jnp.zeros_like(ssq)
        cdt[...] = jnp.zeros_like(cdt)

        def fold(x):
            return sum(x[:, j * HD : (j + 1) * HD] for j in range(per))

        def mixed(o):
            c = cols(o)
            m = mix[:, c] + dot(q_v[:, c], l1[o], 1, 0)
            mix[:, c] = m
            ssq[...] += fold(m * m)
            cdt[...] += fold((gain[:, c] * d_v[:, c].astype(F32)) * m)

        take(p1.at[0 : nc - 1, 0], p1.at[0 : nc - 1, 0], p1_ra)
        mixed(me)

        def mixed_next(i):
            for j in range(1, per):
                back1(i, j).wait_recv()
            mixed(source(i))

        each(nc - 1, mixed_next)

        inv = lax.rsqrt(jnp.sum(ssq[...], 1, keepdims=True) / feat + EPS)
        coef = inv * inv * inv * (jnp.sum(cdt[...], 1, keepdims=True) / feat)

        def post(i):
            o = dest(i)
            c = cols(o)
            m = mix[:, c]
            dy = d_v[:, c].astype(F32)
            g = gain[:, c]
            n = m * inv
            out_v[:, c] = (n * g).astype(BF16)
            gs[o] = jnp.sum(dy * n, 0, keepdims=True)
            d_v[:, c] = (inv * (g * dy) - m * coef).astype(BF16)
            pair_state(q_v, d_v, o, s2)

        def post_send(i):
            post(i)
            out_copy(s2, r2, s2_s, s2_r, i, 0).start()

        each(nc - 1, post_send)
        post(nc - 1)
        for i in others:
            ctx_copy(gs.at[dest(i)], g1.at[me], g1_s, g1_r, i).start()
        for j in range(1, per):
            for i in others:
                out_copy(s2, r2, s2_s, s2_r, i, j).start()
        for j in range(per):
            r2[me, j] = s2[me, j]
        g1[me] = gs[me]

        def grads(o):
            cc = cols(o)
            far = dot(d_v[:, cc], l1[o], 1, 1)
            for j in range(per):
                h = o * per + j
                c = hcols(h)
                dm, k, q = d_v[:, c], k_v[:, c], q_v[:, c]
                w0, w1 = weights(dm, v_v[:, c])
                f = far[:, j * HD : (j + 1) * HD]
                qg_v[:top, c] = (dot(w0, k[:top], 1, 0) + f[:top]).astype(BF16)
                qg_v[top:, c] = (dot(w1, k, 1, 0) + f[top:]).astype(BF16)
                t = dot(w1, q[top:], 0, 0)
                mix[:top, c] = dot(w0, q[:top], 0, 0) + t[:top]
                mix[top:, c] = t[top:]
                t = dot(aw1[h], dm[top:], 0, 0)
                acc[:top, c] = dot(aw0[h], dm[:top], 0, 0) + t[:top]
                acc[top:, c] = t[top:]

        m1, m2 = 7, 14
        each(m1, grads)
        turn(s2, r2, s2_r, back2, p2, l2, 0, True)

        take(gs.at[0 : nc - 1], g1.at[0 : nc - 1], g1_r)
        part = g1[0]
        for c in range(1, nc):
            part = part + g1[c]
        g2s[...] = part
        g2[row] = part

        for i in range(ndp - 1):
            pltpu.make_async_remote_copy(
                src_ref=g2s, dst_ref=g2.at[row], send_sem=g2_s, recv_sem=g2_r,
                device_id={"dp": lax.rem(row + 1 + i, ndp)}, device_id_type=MESH,
            ).start()

        each(m2, grads, m1)

        take(g2.at[0 : ndp - 1], g2.at[0 : ndp - 1], g2_r)
        total = g2[0]
        for c in range(1, ndp):
            total = total + g2[c]
        g3s[...] = total
        g3[me] = total
        for i in others:
            ctx_copy(g3s, g3.at[me], g3_s, g3_r, i).start()

        for j in range(1, per):
            turn(s2, r2, s2_r, back2, p2, l2, j, True)
        each(nc, grads, m2)

        take(g3.at[0 : nc - 1], g3.at[0 : nc - 1], g3_r)
        for c in range(nc):
            gg[:, c * wid : (c + 1) * wid] = g3[c]

        for p, sem in ((s1, s1_s), (p1, p1_s), (s2, s2_s), (p2, p2_s), (g1, g1_s), (g3, g3_s)):
            take(p.at[0 : nc - 1], p.at[0 : nc - 1], sem)
        take(g2.at[0 : ndp - 1], g2.at[0 : ndp - 1], g2_s)
        take(p2.at[0 : nc - 1], p2.at[0 : nc - 1], p2_r)

    bufb = pltpu.VMEM((tok, feat), BF16)
    buff = pltpu.VMEM((tok, feat), F32)
    state = pltpu.VMEM((nc, per, HD, HD), BF16)
    square = pltpu.VMEM((nc, wid, wid), BF16)
    one = pltpu.SemaphoreType.DMA
    part = pltpu.VMEM((1, wid), F32)
    parts = pltpu.VMEM((nc, 1, wid), F32)
    return pl.pallas_call(
        kernel,
        out_shape=(bufb, bufb, buff, buff, bufb, bufb, square, pltpu.VMEM((1, feat), F32)),
        in_specs=[pl.BlockSpec(memory_space=pltpu.MemorySpace.HBM)] * 5,
        out_specs=[pl.BlockSpec(memory_space=pltpu.VMEM)] * 8,
        scratch_shapes=[
            bufb, bufb, pltpu.VMEM((1, feat), F32),
            pltpu.VMEM((heads, top, top), BF16), pltpu.VMEM((heads, low, tok), BF16),
            pltpu.VMEM((tok, HD), F32), pltpu.VMEM((tok, HD), F32),
            state, state, state, square, state, state, state,
            parts, parts, part, pltpu.VMEM((ndp, 1, wid), F32), part, parts,
            one((2, nload)), one, one, one,
            one, one((per,)), one, one, one((per - 1, nc - 1)), one, one((per,)), one, one,
            one, one, one, one, one, one,
        ],
        compiler_params=pltpu.CompilerParams(
            collective_id=0, has_side_effects=True, vmem_limit_bytes=32 * 2**20
        ),
        name="layer",
    )


def make_finish(tok, feat, nc):
    per = feat // HD // nc
    wid = per * HD

    def kernel(out_v, qg_v, mix, acc, k_v, v_v, l2, gg, out_h, qg_h, kg_h, vg_h, gg_o, kg_v, vg_v, sem):
        whole = [
            pltpu.make_async_copy(out_v, out_h, sem.at[0]),
            pltpu.make_async_copy(qg_v, qg_h, sem.at[1]),
            pltpu.make_async_copy(kg_v, kg_h, sem.at[2]),
            pltpu.make_async_copy(vg_v, vg_h, sem.at[3]),
        ]
        whole[0].start()
        whole[1].start()
        gg_o[...] = gg[...]

        def final(o):
            c = pl.ds(pl.multiple_of(o * wid, wid), wid)
            kg_v[:, c] = (mix[:, c] + dot(v_v[:, c], l2[o], 1, 1)).astype(BF16)
            vg_v[:, c] = (acc[:, c] + dot(k_v[:, c], l2[o], 1, 0)).astype(BF16)
            pltpu.make_async_copy(kg_v.at[:, c], kg_h.at[:, c], sem.at[2]).start()
            pltpu.make_async_copy(vg_v.at[:, c], vg_h.at[:, c], sem.at[3]).start()

        each(nc, final)
        for w in whole:
            w.wait()

    big = jax.ShapeDtypeStruct((tok, feat), BF16)
    bufb = pltpu.VMEM((tok, feat), BF16)
    vm = pl.BlockSpec(memory_space=pltpu.VMEM)
    return pl.pallas_call(
        kernel,
        out_shape=(big, big, big, big, jax.ShapeDtypeStruct((1, feat), F32)),
        in_specs=[vm] * 8,
        out_specs=[pl.BlockSpec(memory_space=pltpu.MemorySpace.HBM)] * 4 + [vm],
        scratch_shapes=[bufb, bufb, pltpu.SemaphoreType.DMA((4,))],
        compiler_params=pltpu.CompilerParams(vmem_limit_bytes=12 * 2**20),
        name="finish",
    )


def solution(mesh):
    nc, ndp = mesh.shape["context"], mesh.shape["dp"]

    def shards(queries, keys, values, gain, out_grad):
        tok, feat = queries.shape[1:]
        held = make_layer(tok, feat, nc, ndp)(
            queries[0], keys[0], values[0],
            pltpu.with_memory_space_constraint(gain[None], pltpu.MemorySpace.HBM), out_grad[0],
        )
        out, qg, kg, vg, gg = make_finish(tok, feat, nc)(*held)
        return out[None], qg[None], kg[None], vg[None], gg[0]

    spec = P("dp", "context", None)
    return jax.shard_map(
        shards, mesh=mesh, in_specs=(spec, spec, spec, P(), spec),
        out_specs=(spec, spec, spec, spec, P()), check_vma=False,
    )
```

time: 83.3 us -> 70.1 us (0.84)
  the two profiles are of different devices: /device:TPU:8 before, /device:TPU:1 now
where the time goes in v3:
time: 70.1 us; the launch traced here: 70 us
  Pallas kernels  69.4 us (99%)
    pallas_call x1, Pallas kernels, shards(): make_layer(tok, feat, nc, ndp)  63.6 us
    pallas_call x1, Pallas kernels, shards(): out, qg, kg, vg, gg = make_finish(tok, feat, nc)(*held)  5.77 us

profile of v3, /device:TPU:1, one launch (start us, length us, event | category | flops | bytes accessed | tf_op | source)
XLA Modules:
  0.0 70.0 jit_solution(4276744555751426884)
XLA Ops:
  0.6 63.6 %layer.1 = (bf16[320,4096]{1,0:T(8,128)(2,1)S(1)}, bf16[320,4096]{1,0:T(8,128)(2,1)S(1)}, f32[320,4096]{1,0:T(8,128)S(1)}, f32[320,4096]{1,0:T(8,128)S(1)}, bf16...) custom-call(bf16[320,4096]{1,0:T(8,128)(2,1)} %bitcast.10, ...), custom_call_target="tpu_custom_call" | custom-call | tf_op jit(solution)/shard_map/layer/pallas_call | solution.py:391
  64.3 5.8 %finish.1 = (bf16[320,4096]{1,0:T(8,128)(2,1)}, bf16[320,4096]{1,0:T(8,128)(2,1)}, bf16[320,4096]{1,0:T(8,128)(2,1)}, bf16[320,4096]{1,0:T(8,128)(2,1)}, f32[1,4096]{1,0:T(1,128)}) custom-call(bf16[320,4096]{1,0:T(8,128)(2,1)S(1)} %get-tuple-element.18.out_v, bf16[320,4096]{1,0:T(8,128)(2,1)S(1)} %get-tuple-element.19.qg_v, ...), custom_call_target="tpu_custom_call" | custom-call | tf_op jit(solution)/shard_map/finish/pallas_call | solution.py:395

commit v4 on v3

--- a/solution.py
+++ b/solution.py
@@ -62,7 +62,7 @@
         s1, r1, p1, l1, s2, r2, p2,
         gs, g1, g2s, g2, g3s, g3,
         kv_sem, q_sem, d_sem, gain_sem,
-        s1_s, s1_r, p1_s, p1_ra, p1_rb, s2_s, s2_r, p2_s, p2_r,
+        s1_s, s1_r, p1_s, p1_r, s2_s, s2_r, p2_s, p2_r,
         g1_s, g1_r, g2_s, g2_r, g3_s, g3_r,
     ):
         me = lax.axis_index("context")
@@ -81,19 +81,25 @@
             dz, dy = pick(i, [(nz - s[0]) % nz for s in steps]), pick(i, [(NY - s[1]) % NY for s in steps])
             return lax.rem(mz + dz, nz) * NY + lax.rem(my + dy, NY)
 
+        def kv_load(src, dst, which, i):
+            c = slice(i * lw, (i + 1) * lw)
+            return pltpu.make_async_copy(src.at[:, c], dst.at[:, c], kv_sem.at[which, i])
+
+        def kv_start(i):
+            kv_load(k_h, k_v, 0, i).start()
+            kv_load(v_h, v_v, 1, i).start()
+
+        for i in range(2):
+            kv_start(i)
+
         barrier = pltpu.get_barrier_semaphore()
         for i in others:
             pl.semaphore_signal(barrier, inc=1, device_id={"context": dest(i)}, device_id_type=MESH)
         for i in range(ndp - 1):
             pl.semaphore_signal(barrier, inc=1, device_id={"dp": lax.rem(row + 1 + i, ndp)}, device_id_type=MESH)
 
-        def kv_load(src, dst, which, i):
-            c = slice(i * lw, (i + 1) * lw)
-            return pltpu.make_async_copy(src.at[:, c], dst.at[:, c], kv_sem.at[which, i])
-
-        for i in range(nload):
-            kv_load(k_h, k_v, 0, i).start()
-            kv_load(v_h, v_v, 1, i).start()
+        for i in range(2, nload):
+            kv_start(i)
         q_copy = pltpu.make_async_copy(q_h, q_v, q_sem)
         d_copy = pltpu.make_async_copy(d_h, d_v, d_sem)
         gain_copy = pltpu.make_async_copy(g_h, gain, gain_sem)
@@ -156,7 +162,7 @@
             each(HD // 32, rows32, unroll=2)
 
         def back1(i, j):
-            return back_copy(p1, l1, p1_s, p1_ra if j == 0 else p1_rb.at[j - 1, i], i, j)
+            return back_copy(p1, l1, p1_s, p1_r.at[j], i, j)
 
         def back2(i, j):
             return back_copy(p2, l2, p2_s, p2_r, i, j)
@@ -205,39 +211,40 @@
         ssq[...] = jnp.zeros_like(ssq)
         cdt[...] = jnp.zeros_like(cdt)
 
-        def fold(x):
-            return sum(x[:, j * HD : (j + 1) * HD] for j in range(per))
-
-        def mixed(o):
-            c = cols(o)
-            m = mix[:, c] + dot(q_v[:, c], l1[o], 1, 0)
-            mix[:, c] = m
-            ssq[...] += fold(m * m)
-            cdt[...] += fold((gain[:, c] * d_v[:, c].astype(F32)) * m)
-
-        take(p1.at[0 : nc - 1, 0], p1.at[0 : nc - 1, 0], p1_ra)
-        mixed(me)
-
-        def mixed_next(i):
-            for j in range(1, per):
-                back1(i, j).wait_recv()
-            mixed(source(i))
-
-        each(nc - 1, mixed_next)
+        group = 4
+
+        def mixed(t, j):
+            sq, cd = 0.0, 0.0
+            for k in range(group):
+                o = t * group + k
+                c = hcols(o * per + j)
+                m = mix[:, c] + dot(q_v[:, c], l1[o, j * HD : (j + 1) * HD, j * HD : (j + 1) * HD], 1, 0)
+                mix[:, c] = m
+                sq = sq + m * m
+                cd = cd + (gain[:, c] * d_v[:, c].astype(F32)) * m
+            ssq[...] += sq
+            cdt[...] += cd
+
+        for j in range(per):
+            take(p1.at[0 : nc - 1, j], p1.at[0 : nc - 1, j], p1_r.at[j])
+            each(nc // group, lambda t, j=j: mixed(t, j))
 
         inv = lax.rsqrt(jnp.sum(ssq[...], 1, keepdims=True) / feat + EPS)
         coef = inv * inv * inv * (jnp.sum(cdt[...], 1, keepdims=True) / feat)
+        ssq[...] = jnp.broadcast_to(inv, ssq.shape)
+        cdt[...] = jnp.broadcast_to(coef, cdt.shape)
 
         def post(i):
             o = dest(i)
-            c = cols(o)
-            m = mix[:, c]
-            dy = d_v[:, c].astype(F32)
-            g = gain[:, c]
-            n = m * inv
-            out_v[:, c] = (n * g).astype(BF16)
-            gs[o] = jnp.sum(dy * n, 0, keepdims=True)
-            d_v[:, c] = (inv * (g * dy) - m * coef).astype(BF16)
+            for j in range(per):
+                c = hcols(o * per + j)
+                m = mix[:, c]
+                dy = d_v[:, c].astype(F32)
+                g = gain[:, c]
+                n = m * ssq[...]
+                out_v[:, c] = (n * g).astype(BF16)
+                gs[o, :, j * HD : (j + 1) * HD] = jnp.sum(dy * n, 0, keepdims=True)
+                d_v[:, c] = (ssq[...] * (g * dy) - m * cdt[...]).astype(BF16)
             pair_state(q_v, d_v, o, s2)
 
         def post_send(i):
@@ -273,7 +280,7 @@
                 acc[:top, c] = dot(aw0[h], dm[:top], 0, 0) + t[:top]
                 acc[top:, c] = t[top:]
 
-        m1, m2 = 7, 14
+        m1, m2 = 5, 10
         each(m1, grads)
         turn(s2, r2, s2_r, back2, p2, l2, 0, True)
 
@@ -333,7 +340,7 @@
             state, state, state, square, state, state, state,
             parts, parts, part, pltpu.VMEM((ndp, 1, wid), F32), part, parts,
             one((2, nload)), one, one, one,
-            one, one((per,)), one, one, one((per - 1, nc - 1)), one, one((per,)), one, one,
+            one, one((per,)), one, one((per,)), one, one((per,)), one, one,
             one, one, one, one, one, one,
         ],
         compiler_params=pltpu.CompilerParams(
@@ -365,7 +372,7 @@
             pltpu.make_async_copy(kg_v.at[:, c], kg_h.at[:, c], sem.at[2]).start()
             pltpu.make_async_copy(vg_v.at[:, c], vg_h.at[:, c], sem.at[3]).start()
 
-        each(nc, final)
+        each(nc, final, unroll=2)
         for w in whole:
             w.wait()
 

time: 70.1 us -> 69.6 us (level)
    pallas_call x1, Pallas kernels: 5.77 us -> 4.55 us  [shards(): out, qg, kg, vg, gg = make_finish(tok, feat, nc)(*held)]
where the time goes in v4:
time: 69.6 us; the launch traced here: 69.4 us
  Pallas kernels  68.8 us (99%)
    pallas_call x1, Pallas kernels, shards(): make_layer(tok, feat, nc, ndp)  64.3 us
    pallas_call x1, Pallas kernels, shards(): out, qg, kg, vg, gg = make_finish(tok, feat, nc)(*held)  4.55 us

profile of v4, /device:TPU:1, one launch (start us, length us, event | category | flops | bytes accessed | tf_op | source)
XLA Modules:
  0.0 69.4 jit_solution(8274270967330392485)
XLA Ops:
  0.6 64.3 %layer.1 = (bf16[320,4096]{1,0:T(8,128)(2,1)S(1)}, bf16[320,4096]{1,0:T(8,128)(2,1)S(1)}, f32[320,4096]{1,0:T(8,128)S(1)}, f32[320,4096]{1,0:T(8,128)S(1)}, bf16...) custom-call(bf16[320,4096]{1,0:T(8,128)(2,1)} %bitcast.10, ...), custom_call_target="tpu_custom_call" | custom-call | tf_op jit(solution)/shard_map/layer/pallas_call | solution.py:398
  64.9 4.6 %finish.1 = (bf16[320,4096]{1,0:T(8,128)(2,1)}, bf16[320,4096]{1,0:T(8,128)(2,1)}, bf16[320,4096]{1,0:T(8,128)(2,1)}, bf16[320,4096]{1,0:T(8,128)(2,1)}, f32[1,4096]{1,0:T(1,128)}) custom-call(bf16[320,4096]{1,0:T(8,128)(2,1)S(1)} %get-tuple-element.18.out_v, bf16[320,4096]{1,0:T(8,128)(2,1)S(1)} %get-tuple-element.19.qg_v, ...), custom_call_target="tpu_custom_call" | custom-call | tf_op jit(solution)/shard_map/finish/pallas_call | solution.py:402
